TPU v7x, 512 devices: a whole 4x8x8 slice. The times are simulated.
512 devices in a mesh: tm: 16 (over x, y_hi), chan: 32 (over y_lo, z, core).
Axes of the slice: x: 4, y: 8 (y_hi: 4, y_lo: 2; y = y_hi * 2 + y_lo), z: 8, core: 2. Of those that a mesh axis runs over, the one named last changes fastest.
Arguments:
- latent_input: bfloat16 [2048, 1280], P('chan', 'tm'), may hold values from -6 to 6
- upsample_kernel: bfloat16 [16, 1024, 2048], P(None, 'chan', 'tm'), may hold values from -0.09375 to 0.09375
- dilated_kernel: bfloat16 [2, 7, 1024, 1024], P(None, None, 'chan'), may hold values from -0.0625 to 0.0625
- pointwise_kernel: bfloat16 [2, 1024, 1024], P(None, 'chan'), may hold values from -0.1875 to 0.1875
- dilated_prune_mask: int32 [2, 7, 1024, 128], P(None, None, 'chan'), may hold values 0 or 1
- pointwise_prune_mask: int32 [2, 1024, 128], P(None, 'chan'), may hold values 0 or 1
- snake_freq_upsample: float32 [2048], P('chan'), may hold values from 0.5 to 3
- snake_freq_dilated: float32 [2, 1024], P(None, 'chan'), may hold values from 0.5 to 3
- snake_freq_pointwise: float32 [2, 1024], P(None, 'chan'), may hold values from 0.5 to 3
- segment_lengths: int32 [3], replicated, may hold values from 1 to 720, as said below
- cotangent: bfloat16 [1024, 10240], P('chan', 'tm'), may hold values from -6 to 6
Outputs:
- decoded: bfloat16 [1024, 10240], P('chan', 'tm')
- dil_saliency: float32 [2, 7, 1024, 1024], P(None, None, 'chan')
- point_saliency: float32 [2, 1024, 1024], P(None, 'chan')
Inputs may be any that keep to these rules, and one draw needn't show every extreme that they name: `segment_lengths`: 3 lengths in latent frames that sum to 1280, in an order drawn with them; the longest is exactly 720.
All inputs are finite; a program needn't handle non-finite values. No bound on the sum of `dilated_prune_mask` or of `pointwise_prune_mask` on one device may be relied on, other than what follows from the above.
Results may differ from a plain program's by a relative error of at most 0.035.
Values may be sent and summed in bfloat16 or wider, within the bound.
No kernel may reach another device: no remote copies, remote signals or barrier semaphores. Data moves between devices by JAX's collectives and lax.ppermute only.
A program may use at most 128 MiB of HBM per device.

v0:
```python
import jax
import jax.numpy as jnp
from jax import lax
from jax.sharding import PartitionSpec as P


def with_halo(cells, sides, width):
    for axis, dim in sides:
        count = lax.axis_size(axis)
        ends = count - 1
        head = lax.slice_in_dim(cells, 0, width, axis=dim)
        tail = lax.slice_in_dim(cells, cells.shape[dim] - width, cells.shape[dim], axis=dim)
        cells = jnp.concatenate(
            [
                lax.ppermute(tail, axis, [(i, (i + 1) % count) for i in range(ends)]),
                cells,
                lax.ppermute(head, axis, [((i + 1) % count, i) for i in range(ends)]),
            ],
            axis=dim,
        )
    return cells


def joined_along(tiles, dim):
    shape = list(tiles.shape[1:])
    shape[dim] *= tiles.shape[0]
    return jnp.moveaxis(tiles, 0, dim).reshape(shape)


def copy_for_each(value, axis):
    size = lax.axis_size(axis)
    return lax.all_to_all(
        jnp.broadcast_to(value[None], (size, *value.shape)), axis, 0, 0, tiled=True
    )


def gathered_copies(value, axis, dim):
    return joined_along(copy_for_each(value, axis), dim)


def split_up(value, dim, size):
    before, after = (value.shape[:dim], value.shape[dim + 1 :])
    return jnp.moveaxis(value.reshape(*before, size, -1, *after), dim, 0)


def sum_at_owner(value, axis, dim):
    tiles = split_up(value, dim, lax.axis_size(axis))
    arrived = lax.all_to_all(tiles, axis, split_axis=0, concat_axis=0, tiled=True)
    return arrived.astype(jnp.float32).sum(axis=0)


def snake_act(values, alpha):
    scale = alpha[:, None]
    return values + jnp.sin(scale * values) ** 2 / scale


def snake_slope(values, alpha):
    return 1.0 + jnp.sin(2.0 * alpha[:, None] * values)


def track_ids(lengths, frame_index, total_frames):
    starts = jnp.cumsum(lengths) - lengths
    found = jnp.sum((starts[:, None] <= frame_index[None, :]).astype(jnp.int32), axis=0) - 1
    return jnp.where(frame_index < 0, -1, jnp.where(frame_index >= total_frames, -2, found))


def per_device(
    latent_input,
    upsample_kernel,
    dilated_kernel,
    pointwise_kernel,
    dilated_prune_mask,
    pointwise_prune_mask,
    snake_freq_upsample,
    snake_freq_dilated,
    snake_freq_pointwise,
    segment_lengths,
    cotangent,
):
    stride = upsample_kernel.shape[0] // 2
    half_stride = stride // 2
    frame_count = latent_input.shape[1]
    row_count = frame_count * stride
    total_frames = frame_count * lax.axis_size("tm")
    out_local = upsample_kernel.shape[1]
    residual_unit_count = dilated_kernel.shape[0]
    kernel_tap_count = dilated_kernel.shape[1]
    total_frame_width = dilated_kernel.shape[3]
    prune_block_width = total_frame_width // dilated_prune_mask.shape[3]
    activated = snake_act(latent_input.astype(jnp.float32), snake_freq_upsample).astype(
        jnp.bfloat16
    )
    bordered = with_halo(activated, (("tm", 1),), 1)
    channels_all = gathered_copies(bordered, "chan", 0)
    weight_block = lax.all_gather(upsample_kernel, "tm", axis=2, tiled=True)
    number = weight_block.shape[2]
    middle = jnp.dot(
        weight_block[half_stride : half_stride + stride].reshape(stride * out_local, number),
        channels_all[:, 1:-1],
        preferred_element_type=jnp.float32,
    )
    lower = jnp.dot(
        weight_block[half_stride + stride :].reshape(half_stride * out_local, number),
        channels_all[:, :-2],
        preferred_element_type=jnp.float32,
    )
    upper = jnp.dot(
        weight_block[:half_stride].reshape(half_stride * out_local, number),
        channels_all[:, 2:],
        preferred_element_type=jnp.float32,
    )
    middle, lower, upper = (middle, lower, upper)
    frame_pos = lax.axis_index("tm") * frame_count + jnp.arange(frame_count, dtype=jnp.int32)
    frame_ids = track_ids(segment_lengths, frame_pos, total_frames)
    prev_ok = (frame_ids == track_ids(segment_lengths, frame_pos - 1, total_frames)).astype(
        jnp.float32
    )
    next_ok = (frame_ids == track_ids(segment_lengths, frame_pos + 1, total_frames)).astype(
        jnp.float32
    )
    neighbour = jnp.concatenate(
        [
            (lower * prev_ok[None, :]).reshape(half_stride, out_local, frame_count),
            (upper * next_ok[None, :]).reshape(half_stride, out_local, frame_count),
        ],
        axis=0,
    )
    hidden_state = (
        (middle.reshape(stride, out_local, frame_count) + neighbour)
        .transpose(1, 2, 0)
        .reshape(out_local, row_count)
    )
    row_pos = lax.axis_index("tm") * row_count + jnp.arange(row_count, dtype=jnp.int32)
    own_ids = track_ids(segment_lengths, jnp.floor_divide(row_pos, stride), total_frames)

    def tap_mask(offset):
        other = track_ids(segment_lengths, jnp.floor_divide(row_pos + offset, stride), total_frames)
        return (own_ids == other).astype(jnp.float32)

    saved_residuals = []
    for residual_unit_index in range(residual_unit_count):
        spacing = 3 ** (residual_unit_index + 1)
        margin = 3 * spacing
        dilated_effective = dilated_kernel[residual_unit_index] * jnp.repeat(
            dilated_prune_mask[residual_unit_index], prune_block_width, axis=-1
        ).astype(jnp.bfloat16)
        pointwise_effective = pointwise_kernel[residual_unit_index] * jnp.repeat(
            pointwise_prune_mask[residual_unit_index], prune_block_width, axis=-1
        ).astype(jnp.bfloat16)
        first = snake_act(hidden_state, snake_freq_dilated[residual_unit_index]).astype(
            jnp.bfloat16
        )
        first_wide = with_halo(first, (("tm", 1),), margin)
        padded_input = gathered_copies(first_wide, "chan", 0)
        kernel_tap_masks = jnp.stack(
            [
                tap_mask((kernel_tap_index - 3) * spacing)
                for kernel_tap_index in range(kernel_tap_count)
            ]
        )
        track_window_list = jnp.stack(
            [
                padded_input[:, kernel_tap_index * spacing : kernel_tap_index * spacing + row_count]
                for kernel_tap_index in range(kernel_tap_count)
            ]
        )
        conv_result = jnp.zeros((out_local, row_count), jnp.float32)
        for kernel_tap_index in range(kernel_tap_count):
            conv_result = conv_result + kernel_tap_masks[kernel_tap_index][None, :] * jnp.dot(
                dilated_effective[kernel_tap_index],
                track_window_list[kernel_tap_index],
                preferred_element_type=jnp.float32,
            )
        second_activation = snake_act(
            conv_result, snake_freq_pointwise[residual_unit_index]
        ).astype(jnp.bfloat16)
        second_activation_all = lax.all_gather(second_activation, "chan", axis=0, tiled=True)
        saved_residuals.append(
            (
                hidden_state,
                track_window_list,
                conv_result,
                second_activation_all,
                dilated_effective,
                pointwise_effective,
            )
        )
        hidden_state = hidden_state + jnp.dot(
            pointwise_effective, second_activation_all, preferred_element_type=jnp.float32
        )
    decoded = hidden_state.astype(jnp.bfloat16)
    grad_out = cotangent.astype(jnp.float32)
    dilated_gradient_list = [None] * residual_unit_count
    point_grads = [None] * residual_unit_count
    for residual_unit_index in reversed(range(residual_unit_count)):
        spacing = 3 ** (residual_unit_index + 1)
        margin = 3 * spacing
        (
            hidden_input,
            track_window_list,
            conv_result,
            second_activation_all,
            dilated_effective,
            pointwise_effective,
        ) = saved_residuals[residual_unit_index]
        grad_b = grad_out.astype(jnp.bfloat16)
        pointwise_gradient = lax.dot_general(
            grad_b,
            second_activation_all,
            (((1,), (1,)), ((), ())),
            preferred_element_type=jnp.float32,
        )
        grad_second = sum_at_owner(
            lax.dot_general(
                pointwise_effective,
                grad_b,
                (((0,), (0,)), ((), ())),
                preferred_element_type=jnp.float32,
            ).astype(jnp.bfloat16),
            "chan",
            0,
        )
        grad_conv = (
            grad_second * snake_slope(conv_result, snake_freq_pointwise[residual_unit_index])
        ).astype(jnp.bfloat16)
        src_masks = jnp.stack(
            [
                tap_mask((kernel_tap_index - 3) * spacing)
                for kernel_tap_index in range(kernel_tap_count)
            ]
        )
        masked_kernel = grad_conv[None, :, :] * src_masks[:, None, :].astype(jnp.bfloat16)
        dilated_gradient = lax.dot_general(
            masked_kernel,
            track_window_list,
            (((2,), (2,)), ((0,), (0,))),
            preferred_element_type=jnp.float32,
        )
        dilated_gradient_list[residual_unit_index] = dilated_gradient
        point_grads[residual_unit_index] = pointwise_gradient
        if residual_unit_index > 0:
            grad_wide = with_halo(grad_conv, (("tm", 1),), margin)
            shifted = []
            for kernel_tap_index in range(kernel_tap_count):
                dest_mask = tap_mask(-(kernel_tap_index - 3) * spacing).astype(jnp.bfloat16)
                track_window = grad_wide[
                    :,
                    (6 - kernel_tap_index) * spacing : (6 - kernel_tap_index) * spacing + row_count,
                ]
                shifted.append(track_window * dest_mask[None, :])
            shifted = jnp.stack(shifted)
            grad_first = sum_at_owner(
                lax.dot_general(
                    dilated_effective,
                    shifted,
                    (((0, 1), (0, 1)), ((), ())),
                    preferred_element_type=jnp.float32,
                ).astype(jnp.bfloat16),
                "chan",
                0,
            )
            grad_out = grad_out + grad_first * snake_slope(
                hidden_input, snake_freq_dilated[residual_unit_index]
            )
    dilated_gradient_total, pointwise_gradient_total = (
        lax.psum(jnp.stack(dilated_gradient_list).astype(jnp.bfloat16), "tm").astype(jnp.float32),
        lax.psum(jnp.stack(point_grads).astype(jnp.bfloat16), "tm").astype(jnp.float32),
    )
    dilated_effective_list = jnp.stack([list_entry[4] for list_entry in saved_residuals]).astype(
        jnp.float32
    )
    pointwise_effective_list = jnp.stack([list_entry[5] for list_entry in saved_residuals]).astype(
        jnp.float32
    )
    return (
        decoded,
        dilated_effective_list * dilated_gradient_total,
        pointwise_effective_list * pointwise_gradient_total,
    )


def solution(mesh):
    return jax.shard_map(
        per_device,
        mesh=mesh,
        in_specs=(
            P("chan", "tm"),
            P(None, "chan", "tm"),
            P(None, None, "chan", None),
            P(None, "chan", None),
            P(None, None, "chan", None),
            P(None, "chan", None),
            P("chan"),
            P(None, "chan"),
            P(None, "chan"),
            P(),
            P("chan", "tm"),
        ),
        out_specs=(P("chan", "tm"), P(None, None, "chan", None), P(None, "chan", None)),
        check_vma=False,
    )
```

profile of v0, /device:TPU:1, one launch (start us, length us, event | category | flops | bytes accessed | tf_op | source)
XLA Modules:
  0.0 598.8 jit_solution(14013470186000086537)
XLA Ops:
  8.9 5.0 collective-permute-start
  16.7 3.8 collective-permute-done.1
  21.5 12.5 %all-to-all-start = ((bf16[32,64,82]{2,1,0:T(8,128)(2,1)}), bf16[32,64,82]{2,1,0:T(8,128)(2,1)S(1)}, u32[]{:S(2)}, u32[]{:S(2)}) async-start(bf16[32,64,82]{2,1,0:T(8,128)(2,1)} %broadcast_in_dim.102), calls=%async_computation | async-start | bytes 1048576 | tf_op jit(solution)/shard_map/all_to_all | solution.py:32
  34.6 47.9 %all-gather.4.cloned.1.call-done = bf16[16,32,2048]{2,1,0:T(8,128)(2,1)} async-done(((bf16[16,32,128]{2,1,0:T(8,128)(2,1)}), bf16[16,32,2048]{2,1,0:T(8,128)(2,1)}) %all-gather.4.cloned.1.call-update) | async-done | bytes 2097168 | tf_op jit(solution)/shard_map/all_gather | solution.py:95
  87.7 1.9 collective-permute-start.2
  90.9 4.0 collective-permute-done.3
  96.4 15.4 %all-to-all-start.1 = ((bf16[32,32,658]{2,1,0:T(8,128)(2,1)}), bf16[32,32,658]{2,1,0:T(8,128)(2,1)S(1)}, u32[]{:S(2)}, u32[]{:S(2)}) async-start(bf16[32,32,658]{2,1,0:T(8,128)(2,1)} %broadcast_in_dim.108), calls=%async_computation.1 | async-start | bytes 3145728 | tf_op jit(solution)/shard_map/all_to_all | solution.py:32
  113.6 2.8 broadcast_bitcast_fusion.2
  117.8 2.8 broadcast_bitcast_fusion
  120.6 1.4 copy.87
  123.6 2.3 bitcast_multiply_fusion
  125.9 25.2 %all-to-all-done.1 = bf16[32,32,658]{2,1,0:T(8,128)(2,1)S(1)} async-done(((bf16[32,32,658]{2,1,0:T(8,128)(2,1)}), bf16[32,32,658]{2,1,0:T(8,128)(2,1)S(1)}, u32[]{:S(2)}, u32[]{:S(2)}) %all-to-all-start.1) | async-done | bytes 1347616 | tf_op jit(solution)/shard_map/all_to_all | solution.py:32
  154.4 1.4 add_convert_fusion.3
  156.9 1.6 convolution_convert_fusion.1
  158.5 4.8 all-to-all-start.3
  165.0 68.0 %all-gather.6.cloned.1.call-done = bf16[1024,640]{1,0:T(8,128)(2,1)} async-done(((bf16[32,640]{1,0:T(8,128)(2,1)}), bf16[1024,640]{1,0:T(8,128)(2,1)}) %all-gather.6.cloned.1.call-update) | async-done | bytes 1310736 | tf_op jit(solution)/shard_map/all_gather | solution.py:177
  233.0 1.9 add_convert_fusion.2
  234.9 3.0 collective-permute-start.4
  240.0 3.3 collective-permute-done.5
  243.4 1.5 broadcast_in_dim.111
  244.9 7.9 %all-to-all-start.2 = ((bf16[32,32,694]{2,1,0:T(8,128)(2,1)}), bf16[32,32,694]{2,1,0:T(8,128)(2,1)S(1)}, u32[]{:S(2)}, u32[]{:S(2)}) async-start(bf16[32,32,694]{2,1,0:T(8,128)(2,1)} %broadcast_in_dim.111), calls=%async_computation.2 | async-start | bytes 3145728 | tf_op jit(solution)/shard_map/all_to_all | solution.py:32
  256.4 2.1 convert_reduce_fusion.2
  258.6 33.6 %all-to-all-done.2 = bf16[32,32,694]{2,1,0:T(8,128)(2,1)S(1)} async-done(((bf16[32,32,694]{2,1,0:T(8,128)(2,1)}), bf16[32,32,694]{2,1,0:T(8,128)(2,1)S(1)}, u32[]{:S(2)}, u32[]{:S(2)}) %all-to-all-start.2) | async-done | bytes 1421344 | tf_op jit(solution)/shard_map/all_to_all | solution.py:32
  292.2 1.5 fusion.90
  297.4 1.7 multiply_convert_fusion.1
  301.3 4.9 collective-permute-start.7
  307.3 2.7 bitcast_convert_fusion
  310.0 6.0 all-to-all-start.4
  319.8 3.6 copy-done
  324.5 25.1 %all-to-all-done.4 = bf16[32,32,640]{2,1,0:T(8,128)(2,1)} async-done(((bf16[32,32,640]{2,1,0:T(8,128)(2,1)}), bf16[32,32,640]{2,1,0:T(8,128)(2,1)}, u32[]{:S(2)}, u32[]{:S(2)}) %all-to-all-start.4) | async-done | bytes 1310752 | tf_op jit(solution)/shard_map/all_to_all | solution.py:48
  349.7 1.5 convert_reduce_fusion.1
  351.6 1.7 convolution_convert_fusion
  353.2 5.0 all-to-all-start.5
  358.5 1.6 bitcast_dynamic-update-slice_fusion.5
  360.2 1.7 bitcast_dynamic-update-slice_fusion.4
  361.9 1.6 bitcast_dynamic-update-slice_fusion.3
  363.5 1.6 bitcast_dynamic-update-slice_fusion.2
  365.1 1.6 bitcast_dynamic-update-slice_fusion.1
  366.8 1.6 bitcast_dynamic-update-slice_fusion
  368.4 7.3 %fusion.1 = bf16[1,7,32,1024]{3,2,1,0:T(8,128)(2,1)} fusion(bf16[7,1024,640]{2,1,0:T(8,128)(2,1)} %bitcast_dynamic-update-slice_fusion, bf16[7,640]{1,0:T(8,128)(2,1)S(1)} %stack.162, bf16[32,640]{1,0:T(8,128)(2,1)S(1)} %get-tuple-element.47), kind=kOutput, calls=%fused_computation.24 | convolution fusion | flops 293974016 | bytes 9683712 | tf_op jit(solution)/shard_map/dot_general | solution.py:233
  375.7 35.9 %all-gather.8.cloned.1.call-done = bf16[1024,640]{1,0:T(8,128)(2,1)} async-done(((bf16[32,640]{1,0:T(8,128)(2,1)}), bf16[1024,640]{1,0:T(8,128)(2,1)}) %all-gather.8.cloned.1.call-update) | async-done | bytes 1310736 | tf_op jit(solution)/shard_map/all_gather | solution.py:177
  411.7 1.8 fusion.103
  414.7 1.5 convert_reduce_fusion
  416.6 6.5 %fusion = bf16[1,7,32,1024]{3,2,1,0:T(8,128)(2,1)S(1)} fusion(bf16[7,1024,640]{2,1,0:T(8,128)(2,1)} %copy-done, bf16[7,640]{1,0:T(8,128)(2,1)S(1)} %stack.152, bf16[32,640]{1,0:T(8,128)(2,1)S(1)} %multiply_convert_fusion), kind=kOutput, calls=%fused_computation.23 | convolution fusion | flops 293974016 | bytes 9683712 | tf_op jit(solution)/shard_map/dot_general | solution.py:233
  425.1 1.4 copy.88
  426.5 2.6 copy.89
  432.0 156.8 %all-reduce.3.cloned.1.call-done = (bf16[2,7,32,1024]{3,2,1,0:T(8,128)(2,1)}, bf16[2,32,1024]{2,1,0:T(8,128)(2,1)}) async-done(((bf16[2,7,32,1024]{3,2,1,0:T(8,128)(2,1)}, bf16[2,32,1024]{2,1,0:T(8,128)(2,1)}), (bf16[2,7,32,1024]{3,2,1,0:T(8,128)(2,1)}, bf16[2,32,1024]{2,1,0:T(8,128)(2,1)})) %all-reduce.3.cloned.1.call-update) | async-done | bytes 1048592 | tf_op jit(solution)/shard_map/psum | solution.py:266
  588.8 2.8 convert_multiply_fusion
  (234 shorter events, 49.7 us)
Async XLA Ops:
  7.2 26.9 %copy-start.51 = (f32[2,32]{1,0:T(2,128)S(1)}, f32[2,32]{1,0:T(2,128)}, u32[]{:S(2)}) copy-start(f32[2,32]{1,0:T(2,128)} %param.18) | copy-start | bytes 772
  7.2 75.4 %all-gather.4.cloned.1.call-start = ((), (), s32[]{:S(2)}) async-start(), calls=%async_computation.6 | async-start | bytes 2228224 | tf_op jit(solution)/shard_map/all_gather | solution.py:95
  8.9 7.8 %collective-permute-start = (bf16[64,1]{1,0:T(8,128)(2,1)S(1)}, bf16[64,1]{1,0:T(8,128)(2,1)S(1)}, u32[]{:S(2)}, u32[]{:S(2)}) collective-permute-start(bf16[64,1]{1,0:T(8,128)(2,1)S(1)} %get-tuple-element.61), channel_id=1, source_target_pairs={{0,32},{32,64},{64,96},{96,128},{128,160},{160,192},{192,224},{224... | collective-permute-start | bytes 392 | tf_op jit(solution)/shard_map/ppermute | solution.py:15
  13.9 6.6 %collective-permute-start.1 = (bf16[64,1]{1,0:T(8,128)(2,1)S(1)}, bf16[64,1]{1,0:T(8,128)(2,1)S(1)}, u32[]{:S(2)}, u32[]{:S(2)}) collective-permute-start(bf16[64,1]{1,0:T(8,128)(2,1)S(1)} %get-tuple-element.62), channel_id=1, source_target_pairs={{32,0},{64,32},{96,64},{128,96},{160,128},{192,160},{224,192},{256... | collective-permute-start | bytes 392 | tf_op jit(solution)/shard_map/ppermute | solution.py:17
  21.5 61.1 %all-to-all-start = ((bf16[32,64,82]{2,1,0:T(8,128)(2,1)}), bf16[32,64,82]{2,1,0:T(8,128)(2,1)S(1)}, u32[]{:S(2)}, u32[]{:S(2)}) async-start(bf16[32,64,82]{2,1,0:T(8,128)(2,1)} %broadcast_in_dim.102), calls=%async_computation | async-start | bytes 1048576 | tf_op jit(solution)/shard_map/all_to_all | solution.py:32
  87.3 9.1 %copy-start.13 = (f32[32,640]{1,0:T(8,128)}, f32[32,640]{1,0:T(8,128)S(1)}, u32[]{:S(2)}) copy-start(f32[32,640]{1,0:T(8,128)S(1)} %copy.83) | copy-start | bytes 245764
  87.7 3.2 collective-permute-start.2
  89.6 5.3 collective-permute-start.3
  96.4 15.5 %copy-start.22 = (s32[2,7,32,128]{3,2,1,0:T(8,128)S(1)}, s32[2,7,32,128]{3,2,1,0:T(8,128)}, u32[]{:S(2)}) copy-start(s32[2,7,32,128]{3,2,1,0:T(8,128)} %param.15) | copy-start | bytes 688132
  96.4 54.7 %all-to-all-start.1 = ((bf16[32,32,658]{2,1,0:T(8,128)(2,1)}), bf16[32,32,658]{2,1,0:T(8,128)(2,1)S(1)}, u32[]{:S(2)}, u32[]{:S(2)}) async-start(bf16[32,32,658]{2,1,0:T(8,128)(2,1)} %broadcast_in_dim.108), calls=%async_computation.1 | async-start | bytes 3145728 | tf_op jit(solution)/shard_map/all_to_all | solution.py:32
  111.8 121.1 %all-gather.6.cloned.1.call-start = ((), (), s32[]{:S(2)}) async-start(), calls=%async_computation.7 | async-start | bytes 1351680 | tf_op jit(solution)/shard_map/all_gather | solution.py:177
  122.3 29.3 %copy-start.26 = (s32[640]{0:T(1024)}, s32[640]{0:T(1024)S(1)}, u32[]{:S(2)}) copy-start(s32[640]{0:T(1024)S(1)} %get-tuple-element.8) | copy-start | bytes 7684
  123.6 29.8 %copy-start.29 = (f32[640]{0:T(1024)}, f32[640]{0:T(1024)S(1)}, u32[]{:S(2)}) copy-start(f32[640]{0:T(1024)S(1)} %get-tuple-element.76) | copy-start | bytes 7684
  123.6 30.8 %copy-start.46 = (f32[640]{0:T(1024)}, f32[640]{0:T(1024)S(1)}, u32[]{:S(2)}) copy-start(f32[640]{0:T(1024)S(1)} %get-tuple-element.68) | copy-start | bytes 7684
  158.5 74.4 %copy-start.14 = (f32[32,640]{1,0:T(8,128)S(1)}, f32[32,640]{1,0:T(8,128)}, u32[]{:S(2)}) copy-start(f32[32,640]{1,0:T(8,128)} %copy-done.13) | copy-start | bytes 245764
  158.5 84.8 %all-to-all-start.3 = ((bf16[32,32,640]{2,1,0:T(8,128)(2,1)}), bf16[32,32,640]{2,1,0:T(8,128)(2,1)S(1)}, u32[]{:S(2)}, u32[]{:S(2)}) async-start(bf16[32,32,640]{2,1,0:T(8,128)(2,1)} %bitcast.234), calls=%async_computation.3 | async-start | bytes 2621440 | tf_op jit(solution)/shard_map/all_to_all | solution.py:48
  234.9 116.3 %copy-start.11 = (f32[32,640]{1,0:T(8,128)}, f32[32,640]{1,0:T(8,128)S(1)}, u32[]{:S(2)}) copy-start(f32[32,640]{1,0:T(8,128)S(1)} %get-tuple-element.97) | copy-start | bytes 245764
  234.9 5.0 collective-permute-start.4
  238.0 5.3 collective-permute-start.5
  244.9 8.6 %copy-start.49 = (f32[2,32]{1,0:T(2,128)S(1)}, f32[2,32]{1,0:T(2,128)}, u32[]{:S(2)}) copy-start(f32[2,32]{1,0:T(2,128)} %param.19) | copy-start | bytes 772
  244.9 47.3 %copy-start.47 = (f32[640]{0:T(1024)S(1)}, f32[640]{0:T(1024)}, u32[]{:S(2)}) copy-start(f32[640]{0:T(1024)} %copy-done.46) | copy-start | bytes 7684
  244.9 47.2 %all-to-all-start.2 = ((bf16[32,32,694]{2,1,0:T(8,128)(2,1)}), bf16[32,32,694]{2,1,0:T(8,128)(2,1)S(1)}, u32[]{:S(2)}, u32[]{:S(2)}) async-start(bf16[32,32,694]{2,1,0:T(8,128)(2,1)} %broadcast_in_dim.111), calls=%async_computation.2 | async-start | bytes 3145728 | tf_op jit(solution)/shard_map/all_to_all | solution.py:32
  252.9 40.8 %copy-start.30 = (f32[640]{0:T(1024)S(1)}, f32[640]{0:T(1024)}, u32[]{:S(2)}) copy-start(f32[640]{0:T(1024)} %copy-done.29) | copy-start | bytes 7684
  258.6 36.5 %copy-start.45 = (f32[640]{0:T(1024)S(1)}, f32[640]{0:T(1024)}, u32[]{:S(2)}) copy-start(f32[640]{0:T(1024)} %get-tuple-element.74) | copy-start | bytes 7684
  296.7 4.3 copy-start.31
  296.7 4.3 copy-start.32
  296.7 4.3 copy-start.33
  296.7 4.3 copy-start.34
  296.7 4.3 copy-start.35
  297.3 3.9 copy-start.36
  297.3 8.9 %copy-start.42 = (bf16[640]{0:T(1024)(128)(2,1)S(1)}, bf16[640]{0:T(1024)(128)(2,1)}, u32[]{:S(2)}) copy-start(bf16[640]{0:T(1024)(128)(2,1)} %get-tuple-element.29) | copy-start | bytes 3844
  297.3 9.0 %copy-start.41 = (bf16[640]{0:T(1024)(128)(2,1)S(1)}, bf16[640]{0:T(1024)(128)(2,1)}, u32[]{:S(2)}) copy-start(bf16[640]{0:T(1024)(128)(2,1)} %get-tuple-element.73) | copy-start | bytes 3844
  297.3 9.1 %copy-start.40 = (bf16[640]{0:T(1024)(128)(2,1)S(1)}, bf16[640]{0:T(1024)(128)(2,1)}, u32[]{:S(2)}) copy-start(bf16[640]{0:T(1024)(128)(2,1)} %get-tuple-element.67) | copy-start | bytes 3844
  297.3 9.7 %copy-start.39 = (bf16[640]{0:T(1024)(128)(2,1)S(1)}, bf16[640]{0:T(1024)(128)(2,1)}, u32[]{:S(2)}) copy-start(bf16[640]{0:T(1024)(128)(2,1)} %get-tuple-element.75) | copy-start | bytes 3844
  297.3 9.7 %copy-start.38 = (bf16[640]{0:T(1024)(128)(2,1)S(1)}, bf16[640]{0:T(1024)(128)(2,1)}, u32[]{:S(2)}) copy-start(bf16[640]{0:T(1024)(128)(2,1)} %get-tuple-element.71) | copy-start | bytes 3844
  297.3 9.8 %copy-start.37 = (bf16[640]{0:T(1024)(128)(2,1)S(1)}, bf16[640]{0:T(1024)(128)(2,1)}, u32[]{:S(2)}) copy-start(bf16[640]{0:T(1024)(128)(2,1)} %get-tuple-element.69) | copy-start | bytes 3844
  299.7 6.5 %collective-permute-start.6 = (bf16[32,27]{1,0:T(8,128)(2,1)}, bf16[32,27]{1,0:T(8,128)(2,1)S(1)}, u32[]{:S(2)}, u32[]{:S(2)}) collective-permute-start(bf16[32,27]{1,0:T(8,128)(2,1)} %get-tuple-element.50), channel_id=1, source_target_pairs={{32,0},{64,32},{96,64},{128,96},{160,128},{192,160},{224,192},{256... | collective-permute-start | bytes 5192 | tf_op jit(solution)/shard_map/ppermute | solution.py:17
  301.3 5.7 collective-permute-start.7
  310.0 6.0 %copy-start.52 = (f32[2,32]{1,0:T(2,128)S(1)}, f32[2,32]{1,0:T(2,128)}, u32[]{:S(2)}) copy-start(f32[2,32]{1,0:T(2,128)} %param.18) | copy-start | bytes 772
  310.0 39.7 %all-to-all-start.4 = ((bf16[32,32,640]{2,1,0:T(8,128)(2,1)}), bf16[32,32,640]{2,1,0:T(8,128)(2,1)}, u32[]{:S(2)}, u32[]{:S(2)}) async-start(bf16[32,32,640]{2,1,0:T(8,128)(2,1)} %bitcast.238), calls=%async_computation.4 | async-start | bytes 2621440 | tf_op jit(solution)/shard_map/all_to_all | solution.py:48
  316.0 95.7 %all-gather.8.cloned.1.call-start = ((), (), s32[]{:S(2)}) async-start(), calls=%async_computation.8 | async-start | bytes 1351680 | tf_op jit(solution)/shard_map/all_gather | solution.py:177
  319.8 3.6 copy-start
  323.4 28.2 %copy-start.17 = (bf16[32,1024]{1,0:T(8,128)(2,1)S(1)}, bf16[32,1024]{1,0:T(8,128)(2,1)}, u32[]{:S(2)}) copy-start(bf16[32,1024]{1,0:T(8,128)(2,1)} %copy.78) | copy-start | bytes 196612
  353.2 61.4 %all-to-all-start.5 = ((bf16[32,32,640]{2,1,0:T(8,128)(2,1)}), bf16[32,32,640]{2,1,0:T(8,128)(2,1)}, u32[]{:S(2)}, u32[]{:S(2)}) async-start(bf16[32,32,640]{2,1,0:T(8,128)(2,1)} %bitcast.58), calls=%async_computation.5 | async-start | bytes 2621440 | tf_op jit(solution)/shard_map/all_to_all | solution.py:48
  358.3 230.5 %all-reduce.3.cloned.1.call-start = ((), (), s32[]{:S(2)}) async-start(), calls=%async_computation.9 | async-start | bytes 2097152 | tf_op jit(solution)/shard_map/psum | solution.py:266
  368.4 45.1 %copy-start.2 = (bf16[1024,640]{1,0:T(8,128)(2,1)S(1)}, bf16[1024,640]{1,0:T(8,128)(2,1)}, u32[]{:S(2)}) copy-start(bf16[1024,640]{1,0:T(8,128)(2,1)} %all-gather.6.cloned.1.call-done) | copy-start | bytes 3932164
  416.6 6.5 %copy-start.6 = (bf16[1,7,32,1024]{3,2,1,0:T(8,128)(2,1)S(1)}, bf16[1,7,32,1024]{3,2,1,0:T(8,128)(2,1)}, u32[]{:S(2)}) copy-start(bf16[1,7,32,1024]{3,2,1,0:T(8,128)(2,1)} %fusion.1) | copy-start | bytes 1376260
  426.5 3.2 copy-start.5
  (26 other events, 50.3 us)
Sparse Core Ops, SparseCore 0:
  11.0 71.5 all-gather.3
  156.0 76.9 all-gather.5
  323.5 88.1 all-gather.7
  424.3 164.4 all-reduce.2
where the time goes:
time: 610 us; the launch traced here: 599 us
  waiting for transfers between devices  405 us (66%)
  starting transfers between devices  72 us (12%)
  local copies, waits for them, and re-layouts  45.3 us (7%)
  matrix products  37.6 us (6%)
  other arithmetic  24.3 us (4%)
  between operations  14.9 us (2%)
    psum x1, waiting for transfers between devices, per_device(): lax.psum(jnp.stack(dilated_gradient_list).astype(jnp.bfloat16), 'tm')  157 us
    all_gather x2, waiting for transfers between devices, per_device(): lax.all_gather(second_activation, 'chan', axis=0, tiled=True)  104 us
    all_to_all x3, waiting for transfers between devices, copy_for_each(): lax.all_to_all(jnp.broadcast_to(value[None], (size, *value.shape)), axis,...  58.7 us
    all_gather x1, waiting for transfers between devices, per_device(): weight_block = lax.all_gather(upsample_kernel, 'tm', axis=2, tiled=True)  47.9 us
    all_to_all x3, starting transfers between devices, copy_for_each(): lax.all_to_all(jnp.broadcast_to(value[None], (size, *value.shape)), axis,...  35.8 us
    all_to_all x3, waiting for transfers between devices, sum_at_owner(): lax.all_to_all(tiles, axis, split_axis=0, concat_axis=0, tiled=True)  25.1 us
    unnamed x123, local copies, waits for them, and re-layouts  16.4 us
    all_to_all x3, starting transfers between devices, sum_at_owner(): lax.all_to_all(tiles, axis, split_axis=0, concat_axis=0, tiled=True)  15.7 us
  transfers between devices with their start and end apart: 18, of which 11 were waited for; matrix products, arithmetic and copies ran while one was open for 11% of the time, Pallas kernels for 0%

commit v1 on v0

v1 whole, which is shorter than its diff:
```python
import jax
import jax.numpy as jnp
from jax import lax
from jax.sharding import Mesh, PartitionSpec as P

TM = ("x", "yh")
CHAN = ("yl", "z", "k")
QUAD = ("yl", "k")
SLOT = ("x", "yh", "yl", "k")
EDGE_FRAMES = 5
EXT_UP = 40
EXT_MID = 28
EXT_GRAD = 40
EXT_BACK = 12
f32 = jnp.float32
bf16 = jnp.bfloat16


def exchange(pieces, axes):
    return lax.all_to_all(pieces, axes, 0, 0, tiled=True)


def copies(value, axes):
    size = lax.axis_size(axes)
    return exchange(jnp.broadcast_to(value[None], (size, *value.shape)), axes)


def shift_pairs(axes, step):
    size = lax.axis_size(axes)
    return [(i, i + step) for i in range(size) if 0 <= i + step < size]


def from_before(value, axes):
    return lax.ppermute(value, axes, shift_pairs(axes, 1))


def from_after(value, axes):
    return lax.ppermute(value, axes, shift_pairs(axes, -1))


def snake_act(values, alpha):
    return values + jnp.sin(alpha * values) ** 2 / alpha


def snake_slope(values, alpha):
    return 1.0 + jnp.sin(2.0 * alpha * values)


def all_channels(blocks):
    return blocks.transpose(1, 0, 2).reshape(blocks.shape[1], -1)


def per_device(
    latent_input,
    upsample_kernel,
    dilated_kernel,
    pointwise_kernel,
    dilated_prune_mask,
    pointwise_prune_mask,
    snake_freq_upsample,
    snake_freq_dilated,
    snake_freq_pointwise,
    segment_lengths,
    cotangent,
):
    taps2, width, cols = upsample_kernel.shape
    stride = taps2 // 2
    frames = latent_input.shape[1]
    tm_size = lax.axis_size(TM)
    quad = lax.axis_size(QUAD)
    z_size = lax.axis_size("z")
    y_size = lax.axis_size("yl")
    total_frames = frames * tm_size
    slot_latent = frames // quad
    slot = slot_latent * stride
    units, taps, _, channels = dilated_kernel.shape
    block = quad * width
    tm_index = lax.axis_index(TM)
    slot_start = (tm_index * quad + lax.axis_index(QUAD)) * slot

    starts = jnp.cumsum(segment_lengths) - segment_lengths

    def ids_of(latent_frame):
        found = jnp.sum((starts[:, None] <= latent_frame[None, :]).astype(jnp.int32), axis=0) - 1
        return jnp.where(
            latent_frame < 0, -1, jnp.where(latent_frame >= total_frames, -2, found)
        )

    def tap_masks(extent, spacing, sign, start):
        rows = start + jnp.arange(-extent, slot + extent, dtype=jnp.int32)
        own = ids_of(jnp.floor_divide(rows, stride))
        return [
            own == ids_of(jnp.floor_divide(rows + sign * (tap - 3) * spacing, stride))
            for tap in range(taps)
        ]

    def pruned(kernel, mask):
        lanes = mask.shape[-1]
        group = jnp.arange(channels, dtype=jnp.int32) // (channels // lanes)
        expand = (jnp.arange(lanes, dtype=jnp.int32)[:, None] == group[None, :]).astype(bf16)
        rows = mask.astype(bf16).reshape(-1, lanes)
        wide_mask = jnp.dot(rows, expand, preferred_element_type=f32).astype(bf16)
        return (kernel.reshape(-1, channels) * wide_mask).reshape(kernel.shape)

    lane = jnp.arange(channels, dtype=jnp.int32)
    part = channels // (z_size * y_size)
    source = (lane // part) % y_size * (z_size * part) + lane // (y_size * part) * part + lane % part
    reorder = (lane[:, None] == source[None, :]).astype(bf16)

    def z_first(value):
        return jnp.dot(value.reshape(-1, channels), reorder, preferred_element_type=f32).astype(bf16).reshape(value.shape)

    def natural(value):
        return lax.dot_general(
            value, reorder, (((1,), (1,)), ((), ())), preferred_element_type=f32
        ).astype(bf16)

    def over_quad(value, axis):
        def spread(value, name, axis):
            both = lax.ppermute(value, name, [(0, 1), (1, 0)])
            pick = (jnp.arange(2, dtype=jnp.int32) == lax.axis_index(name)).reshape(
                (1,) * axis + (2,) + (1,) * (value.ndim - axis)
            )
            return jnp.where(pick, jnp.expand_dims(value, axis), jnp.expand_dims(both, axis))

        out = spread(spread(value, "yl", axis), "k", axis + 1)
        return out.reshape(*value.shape[:axis], quad, *value.shape[axis:])

    x_size = lax.axis_size("x")
    margin = EDGE_FRAMES + 1
    span = frames + 2 * margin
    kernel_yh = copies(upsample_kernel.reshape(taps2 * width, cols), "yh")
    wide = jnp.concatenate(
        [
            from_before(latent_input[:, -margin:], TM),
            latent_input,
            from_after(latent_input[:, :margin], TM),
        ],
        axis=1,
    )
    wide = snake_act(wide.astype(f32), snake_freq_upsample[:, None]).astype(bf16)
    inputs_all = copies(wide, CHAN)
    inputs_x = exchange(inputs_all.reshape(x_size, -1, span), "x")
    inputs_x = inputs_x.reshape(x_size, -1, cols, span)
    mixed = jnp.einsum("xmit,moi->xto", inputs_x, kernel_yh, preferred_element_type=f32)
    half = stride // 2 * width
    wide_latent = slot_latent + 2 * EDGE_FRAMES
    freqs = jnp.concatenate([snake_freq_dilated, snake_freq_pointwise]).reshape(1, -1)
    freqs = jnp.pad(freqs, ((0, 0), (0, stride * width - freqs.shape[1])))
    thirds = []
    for _ in range(3):
        thirds.append(lax.reduce_precision(freqs, 8, 7))
        freqs = freqs - thirds[-1]
    thirds = jnp.concatenate(thirds).astype(bf16)
    pieces = []
    for xi in range(x_size):
        index = xi * lax.axis_size("yh") + lax.axis_index("yh")
        lat = index * frames + jnp.arange(-EDGE_FRAMES, frames + EDGE_FRAMES, dtype=jnp.int32)
        here = ids_of(lat)
        prev_ok = (here == ids_of(lat - 1)).astype(f32)[:, None]
        next_ok = (here == ids_of(lat + 1)).astype(f32)[:, None]
        part = mixed[xi]
        up = jnp.concatenate(
            [
                part[1:-1, half : 2 * half] + prev_ok * part[:-2, 3 * half :],
                part[1:-1, 2 * half : 3 * half] + next_ok * part[2:, :half],
            ],
            axis=1,
        ).astype(bf16)
        for q in range(quad):
            pieces.append(
                jnp.concatenate([up[q * slot_latent : q * slot_latent + wide_latent], thirds])
            )
    arrived = exchange(jnp.stack(pieces), ("x", "yl", "k"))
    arrived = arrived.reshape(x_size, quad, wide_latent + 3, stride * width).astype(f32)
    hidden = (
        arrived[:, :, :wide_latent]
        .sum(axis=0)
        .reshape(quad, wide_latent, stride, width)
        .transpose(1, 2, 0, 3)
        .reshape(wide_latent * stride, block)
    )
    freqs = arrived[0, :, wide_latent:, : 2 * units * width].sum(axis=1)
    freqs = freqs.reshape(quad, 2 * units, width).transpose(1, 0, 2).reshape(2 * units, 1, block)
    freq_dil, freq_point = freqs[:units], freqs[units:]

    dil_eff = pruned(dilated_kernel, dilated_prune_mask)
    point_eff = pruned(pointwise_kernel, pointwise_prune_mask)
    w_point = copies(z_first(point_eff), QUAD)
    w_point = w_point.transpose(1, 0, 2, 3).reshape(units, block, channels)
    dil_z = z_first(dil_eff)
    w_dil = [over_quad(dil_z[u], 1).reshape(taps * block, channels) for u in range(units)]

    cot = exchange(
        cotangent.reshape(width, quad, slot).transpose(1, 0, 2), QUAD
    ).reshape(block, slot).T

    def to_owner(partial):
        rows = partial.shape[0]
        pieces = partial.astype(bf16).reshape(rows, z_size, block).transpose(1, 0, 2)
        return exchange(pieces, "z").astype(f32).sum(axis=0)

    grad_second1 = to_owner(jnp.dot(cot, w_point[1], preferred_element_type=f32))
    hidden, grad_second1 = lax.optimization_barrier((hidden, grad_second1))

    def conv(inputs, weights, masks, first_row, spacing, rows):
        full = lax.dot_general(
            inputs, weights, (((1,), (1,)), ((), ())), preferred_element_type=f32
        )
        total = 0.0
        for tap in range(taps):
            begin = first_row + tap * spacing
            part = full[begin : begin + rows, tap * block : (tap + 1) * block]
            total = total + jnp.where(masks[tap][:, None], part, 0.0)
        return total

    rows0 = slot + 2 * EXT_MID
    first0 = snake_act(hidden, freq_dil[0]).astype(bf16)
    first0_blocks = copies(first0, "z")
    first0_all = all_channels(first0_blocks)
    conv0 = conv(
        first0_all,
        w_dil[0],
        tap_masks(EXT_MID, 3, 1, slot_start),
        EXT_UP - EXT_MID - 9,
        3,
        rows0,
    )
    second0 = snake_act(conv0, freq_point[0]).astype(bf16)
    second0_all = all_channels(copies(second0, "z"))
    gap = EXT_UP - EXT_MID
    hidden1 = hidden[gap : gap + rows0] + lax.dot_general(
        second0_all, w_point[0], (((1,), (1,)), ((), ())), preferred_element_type=f32
    )
    first1 = snake_act(hidden1, freq_dil[1]).astype(bf16)
    first1_blocks = copies(first1, "z")
    first1_all = all_channels(first1_blocks)
    conv1 = conv(
        first1_all,
        w_dil[1],
        tap_masks(0, 9, 1, slot_start),
        EXT_MID - 27,
        9,
        slot,
    )
    second1 = snake_act(conv1, freq_point[1]).astype(bf16)
    second1_all = all_channels(copies(second1, "z"))
    decoded_block = hidden1[EXT_MID : EXT_MID + slot] + lax.dot_general(
        second1_all, w_point[1], (((1,), (1,)), ((), ())), preferred_element_type=f32
    )
    decoded = (
        exchange(decoded_block.astype(bf16).T.reshape(quad, width, slot), QUAD)
        .transpose(1, 0, 2)
        .reshape(width, quad * slot)
    )

    grad_conv1 = (grad_second1 * snake_slope(conv1, freq_point[1])).astype(bf16)
    side = 16
    both = jnp.concatenate([grad_conv1[-EXT_GRAD:], cot[-side:]])
    before = from_before(both, SLOT)
    both = jnp.concatenate([grad_conv1[:EXT_GRAD], cot[:side]])
    after = from_after(both, SLOT)
    grad_conv1 = jnp.concatenate([before[:EXT_GRAD], grad_conv1, after[:EXT_GRAD]])
    cot_wide = jnp.concatenate(
        [before[EXT_GRAD + side - EXT_BACK :], cot, after[EXT_GRAD : EXT_GRAD + EXT_BACK]]
    )
    rows_back = slot + 2 * EXT_BACK
    masks = tap_masks(EXT_BACK, 9, -1, slot_start)
    windows = []
    for tap in range(taps):
        begin = EXT_GRAD - EXT_BACK - 9 * (tap - 3)
        part = grad_conv1[begin : begin + rows_back]
        windows.append(jnp.where(masks[tap][:, None], part, jnp.zeros((), bf16)))
    windows = jnp.concatenate(windows, axis=1)
    grad_first1 = to_owner(jnp.dot(windows, w_dil[1], preferred_element_type=f32))
    skip = EXT_MID - EXT_BACK
    grad_out0 = cot_wide.astype(f32) + grad_first1 * snake_slope(
        hidden1[skip : skip + rows_back], freq_dil[1]
    )
    grad_b0 = grad_out0.astype(bf16)
    grad_second0 = to_owner(jnp.dot(grad_b0, w_point[0], preferred_element_type=f32))
    grad_conv0 = (
        grad_second0 * snake_slope(conv0[skip : skip + rows_back], freq_point[0])
    ).astype(bf16)

    def dil_gradient(grad_conv, extent, spacing, inputs):
        rows = grad_conv.shape[0]
        mine = exchange(grad_conv.T.reshape(quad, width, rows), QUAD)
        parts = []
        for q in range(quad):
            masks = tap_masks(0, spacing, -1, (tm_index * quad + q) * slot)
            row = []
            for tap in range(taps):
                begin = extent - spacing * (tap - 3)
                part = mine[q, :, begin : begin + slot]
                row.append(jnp.where(masks[tap][None, :], part, jnp.zeros((), bf16)))
            parts.append(jnp.concatenate(row, axis=0))
        left = jnp.concatenate(parts, axis=1)
        return jnp.dot(left, inputs, preferred_element_type=f32).astype(bf16)

    def over_time(value):
        rows = value.shape[0]
        arrived = exchange(value.reshape(tm_size, rows // tm_size, channels), TM)
        total = natural(arrived.astype(f32).sum(axis=0).astype(bf16))
        return copies(total, TM).reshape(rows, channels)

    def point_gradient(grad_b, second):
        partial = lax.dot_general(
            grad_b, second, (((0,), (0,)), ((), ())), preferred_element_type=f32
        ).astype(bf16)
        arrived = exchange(partial.reshape(quad, width, channels), QUAD)
        return arrived.astype(f32).sum(axis=0).astype(bf16)

    inputs0 = over_quad(first0_all[EXT_UP : EXT_UP + slot], 0).reshape(quad * slot, channels)
    inputs1 = over_quad(first1_all[EXT_MID : EXT_MID + slot], 0).reshape(quad * slot, channels)
    wide_gc1 = grad_conv1[EXT_GRAD - EXT_MID : EXT_GRAD + slot + EXT_MID]
    dil1 = dil_gradient(wide_gc1, EXT_MID, 9, inputs1)
    point1 = point_gradient(cot, second1_all)
    total1 = over_time(jnp.concatenate([dil1, point1]))
    point0 = point_gradient(
        grad_b0[EXT_BACK : EXT_BACK + slot], second0_all[EXT_MID : EXT_MID + slot]
    )
    dil0 = dil_gradient(grad_conv0, EXT_BACK, 3, inputs0)
    dil0, total1 = lax.optimization_barrier((dil0, total1))
    total0 = over_time(jnp.concatenate([dil0, point0]))
    cut = taps * width
    dil_total = jnp.stack([total0[:cut], total1[:cut]]).reshape(units, taps, width, channels)
    point_total = jnp.stack([total0[cut:], total1[cut:]])
    return (
        decoded,
        dil_eff.astype(f32) * dil_total.astype(f32),
        point_eff.astype(f32) * point_total.astype(f32),
    )


def solution(mesh):
    fine = Mesh(mesh.devices.reshape(4, 4, 2, 8, 2), ("x", "yh", "yl", "z", "k"))
    return jax.shard_map(
        per_device,
        mesh=fine,
        in_specs=(
            P(CHAN, TM),
            P(None, CHAN, TM),
            P(None, None, CHAN, None),
            P(None, CHAN, None),
            P(None, None, CHAN, None),
            P(None, CHAN, None),
            P(CHAN),
            P(None, CHAN),
            P(None, CHAN),
            P(),
            P(CHAN, TM),
        ),
        out_specs=(P(CHAN, TM), P(None, None, CHAN, None), P(None, CHAN, None)),
        check_vma=False,
    )
```

time: 610 us -> 405 us (0.66); the launches traced: 599 us -> 402 us
  waiting for transfers between devices: 405 us -> 150 us
  starting transfers between devices: 72 us -> 158 us
  other arithmetic: 24.3 us -> 48.7 us
  local copies, waits for them, and re-layouts: 45.3 us -> 24.7 us
  matrix products: 37.6 us -> 17.2 us
  between operations: 14.9 us -> 3.32 us
    psum x1 -> x0, waiting for transfers between devices: 157 us -> none  [per_device(): lax.psum(jnp.stack(dilated_gradient_list).astype(jnp.bfloat16), 'tm')]
    all_gather x3 -> x0, waiting for transfers between devices: 152 us -> none  [the longest x2 104 us: per_device(): lax.all_gather(second_activation, 'chan', axis=0, tiled=True)]
    all_to_all x6 -> x22, starting transfers between devices: 51.6 us -> 120 us  [exchange(): return lax.all_to_all(pieces, axes, 0, 0, tiled=True)]
    all_to_all x6 -> x22, waiting for transfers between devices: 83.9 us -> 149 us  [exchange(): return lax.all_to_all(pieces, axes, 0, 0, tiled=True)]
    dot_general x26 -> x18, matrix products: 37.6 us -> 17.2 us  [the longest x2 3.77 us: dil_gradient(): return jnp.dot(left, inputs, preferred_element_type=f32).astype(bf16)]
    ppermute x8 -> x12, starting transfers between devices: 20 us -> 38.4 us  [the longest x8 20 us: spread(): both = lax.ppermute(value, name, [(0, 1), (1, 0)])]
    convert_element_type x16 -> x0, local copies, waits for them, and re-layouts: 17.7 us -> none  [the longest x8 14.2 us: per_device(): dilated_effective = dilated_kernel[residual_unit_index] * jnp.repeat(dila...]
    unnamed x5 -> x29, other arithmetic: 0.44 us -> 15 us
  transfers between devices with their start and end apart: 18 -> 34, of which waited for: 11 -> 19; matrix products, arithmetic and copies ran while one was open for 11% -> 18% of each run, Pallas kernels for 0% -> 0%
where the time goes in v1:
time: 405 us; the launch traced here: 402 us
  starting transfers between devices  158 us (39%)
  waiting for transfers between devices  150 us (37%)
  other arithmetic  48.7 us (12%)
  local copies, waits for them, and re-layouts  24.7 us (6%)
  matrix products  17.2 us (4%)
    all_to_all x22, waiting for transfers between devices, exchange(): return lax.all_to_all(pieces, axes, 0, 0, tiled=True)  149 us
    all_to_all x22, starting transfers between devices, exchange(): return lax.all_to_all(pieces, axes, 0, 0, tiled=True)  120 us
    ppermute x8, starting transfers between devices, spread(): both = lax.ppermute(value, name, [(0, 1), (1, 0)])  20 us
    unnamed x29, other arithmetic  15 us
    ppermute x2, starting transfers between devices, from_before(): return lax.ppermute(value, axes, shift_pairs(axes, 1))  11.3 us
    select_n x5, other arithmetic, spread(): jnp.where(pick, jnp.expand_dims(value, axis), jnp.expand_dims(both, axis))  9.91 us
  transfers between devices with their start and end apart: 34, of which 19 were waited for; matrix products, arithmetic and copies ran while one was open for 18% of the time, Pallas kernels for 0%

profile of v1, /device:TPU:1, one launch (start us, length us, event | category | flops | bytes accessed | tf_op | source)
XLA Modules:
  0.0 401.8 jit_solution(10434410147916171858)
XLA Ops:
  2.8 5.7 %collective-permute-start = (bf16[64,6]{1,0:T(8,128)(2,1)S(1)}, bf16[64,6]{1,0:T(8,128)(2,1)S(1)}, u32[]{:S(2)}, u32[]{:S(2)}) collective-permute-start(bf16[64,6]{1,0:T(8,128)(2,1)S(1)} %get-tuple-element.184), channel_id=1, source_target_pairs={{0,32},{32,64},{64,96},{96,128},{128,160},{160,192},{192,224},{224... | collective-permute-start | bytes 2312 | tf_op jit(solution)/shard_map/ppermute | solution.py:34
  10.0 9.9 %all-to-all-start.5 = ((bf16[4,32,160]{2,1,0:T(8,128)(2,1)}), bf16[4,32,160]{2,1,0:T(8,128)(2,1)S(1)}, u32[]{:S(2)}, u32[]{:S(2)}) async-start(bf16[4,32,160]{2,1,0:T(8,128)(2,1)} %bitcast.574), calls=%async_computation.5 | async-start | bytes 131072 | tf_op jit(solution)/shard_map/all_to_all | solution.py:20
  23.8 3.3 collective-permute-start.2
  27.1 2.0 collective-permute-start.4
  33.2 7.1 %all-to-all-start = ((bf16[32,64,92]{2,1,0:T(8,128)(2,1)}), bf16[32,64,92]{2,1,0:T(8,128)(2,1)S(1)}, u32[]{:S(2)}, u32[]{:S(2)}) async-start(bf16[32,64,92]{2,1,0:T(8,128)(2,1)} %broadcast_in_dim.1202), calls=%async_computation | async-start | bytes 1048576 | tf_op jit(solution)/shard_map/all_to_all | solution.py:20
  42.4 14.3 %all-to-all-done = bf16[32,64,92]{2,1,0:T(8,128)(2,1)S(1)} async-done(((bf16[32,64,92]{2,1,0:T(8,128)(2,1)}), bf16[32,64,92]{2,1,0:T(8,128)(2,1)S(1)}, u32[]{:S(2)}, u32[]{:S(2)}) %all-to-all-start) | async-done | bytes 376864 | tf_op jit(solution)/shard_map/all_to_all | solution.py:20
  57.5 4.3 %all-to-all-start.4 = ((bf16[4,2,32,1024]{3,2,1,0:T(8,128)(2,1)}), bf16[4,2,32,1024]{3,2,1,0:T(8,128)(2,1)S(1)}, u32[]{:S(2)}, u32[]{:S(2)}) async-start(bf16[4,2,32,1024]{3,2,1,0:T(8,128)(2,1)} %broadcast_in_dim.1208), calls=%async_computation.4 | async-start | bytes 1048576 | tf_op jit(solution)/shard_map/all_to_all | solution.py:20
  64.4 5.3 %all-to-all-done.4 = bf16[4,2,32,1024]{3,2,1,0:T(8,128)(2,1)S(1)} async-done(((bf16[4,2,32,1024]{3,2,1,0:T(8,128)(2,1)}), bf16[4,2,32,1024]{3,2,1,0:T(8,128)(2,1)S(1)}, u32[]{:S(2)}, u32[]{:S(2)}) %all-to-all-start.4) | async-done | bytes 524320 | tf_op jit(solution)/shard_map/all_to_all | solution.py:20
  69.7 5.3 %all-to-all-start.1 = ((bf16[4,512,92]{1,2,0:T(8,128)(2,1)}), bf16[4,512,92]{1,2,0:T(8,128)(2,1)S(1)}, u32[]{:S(2)}, u32[]{:S(2)}) async-start(bf16[4,512,92]{1,2,0:T(8,128)(2,1)} %copy.80), calls=%async_computation.1 | async-start | bytes 786432 | tf_op jit(solution)/shard_map/all_to_all | solution.py:20
  75.6 6.0 %all-to-all-done.1 = bf16[4,512,92]{1,2,0:T(8,128)(2,1)S(1)} async-done(((bf16[4,512,92]{1,2,0:T(8,128)(2,1)}), bf16[4,512,92]{1,2,0:T(8,128)(2,1)S(1)}, u32[]{:S(2)}, u32[]{:S(2)}) %all-to-all-start.1) | async-done | bytes 376864 | tf_op jit(solution)/shard_map/all_to_all | solution.py:20
  82.5 6.0 %all-to-all-start.2 = ((bf16[4,512,128]{2,1,0:T(8,128)(2,1)}), bf16[4,512,128]{2,1,0:T(8,128)(2,1)S(1)}, u32[]{:S(2)}, u32[]{:S(2)}) async-start(bf16[4,512,128]{2,1,0:T(8,128)(2,1)} %broadcast_in_dim.1204), calls=%async_computation.2 | async-start | bytes 1048576 | tf_op jit(solution)/shard_map/all_to_all | solution.py:20
  91.1 9.8 %all-to-all-done.2 = bf16[4,512,128]{2,1,0:T(8,128)(2,1)S(1)} async-done(((bf16[4,512,128]{2,1,0:T(8,128)(2,1)}), bf16[4,512,128]{2,1,0:T(8,128)(2,1)S(1)}, u32[]{:S(2)}, u32[]{:S(2)}) %all-to-all-start.2) | async-done | bytes 524320 | tf_op jit(solution)/shard_map/all_to_all | solution.py:20
  100.9 3.7 all-to-all-start.6
  115.3 9.6 %all-to-all-start.3 = ((bf16[16,33,256]{2,1,0:T(8,128)(2,1)}), bf16[16,33,256]{2,1,0:T(8,128)(2,1)S(1)}, u32[]{:S(2)}, u32[]{:S(2)}) async-start(bf16[16,33,256]{2,1,0:T(8,128)(2,1)} %constant_dynamic-update-slice_fusion), calls=%async_computation.3 | async-start | bytes 655360 | tf_op jit(solution)/shard_map/all_to_all | solution.py:20
  128.4 2.3 collective-permute-start.5
  134.9 5.9 %all-to-all-start.7 = ((bf16[8,240,128]{2,1,0:T(8,128)(2,1)}), bf16[8,240,128]{2,1,0:T(8,128)(2,1)S(1)}, u32[]{:S(2)}, u32[]{:S(2)}) async-start(bf16[8,240,128]{2,1,0:T(8,128)(2,1)} %broadcast_in_dim.1211), calls=%async_computation.7 | async-start | bytes 983040 | tf_op jit(solution)/shard_map/all_to_all | solution.py:20
  143.6 3.3 broadcast_select_fusion.1
  147.5 9.2 %all-to-all-done.7 = bf16[8,240,128]{2,1,0:T(8,128)(2,1)S(1)} async-done(((bf16[8,240,128]{2,1,0:T(8,128)(2,1)}), bf16[8,240,128]{2,1,0:T(8,128)(2,1)S(1)}, u32[]{:S(2)}, u32[]{:S(2)}) %all-to-all-start.7) | async-done | bytes 491552 | tf_op jit(solution)/shard_map/all_to_all | solution.py:20
  160.5 3.6 all-to-all-start.8
  167.4 10.6 %all-to-all-done.8 = bf16[8,216,128]{2,1,0:T(8,128)(2,1)S(1)} async-done(((bf16[8,216,128]{2,1,0:T(8,128)(2,1)}), bf16[8,216,128]{2,1,0:T(8,128)(2,1)S(1)}, u32[]{:S(2)}, u32[]{:S(2)}) %all-to-all-start.8) | async-done | bytes 442400 | tf_op jit(solution)/shard_map/all_to_all | solution.py:20
  180.0 4.1 %all-to-all-start.9 = ((bf16[8,216,128]{2,1,0:T(8,128)(2,1)}), bf16[8,216,128]{2,1,0:T(8,128)(2,1)}, u32[]{:S(2)}, u32[]{:S(2)}) async-start(bf16[8,216,128]{2,1,0:T(8,128)(2,1)} %broadcast_in_dim.1228), calls=%async_computation.9 | async-start | bytes 884736 | tf_op jit(solution)/shard_map/all_to_all | solution.py:20
  187.3 9.5 %all-to-all-done.9 = bf16[8,216,128]{2,1,0:T(8,128)(2,1)} async-done(((bf16[8,216,128]{2,1,0:T(8,128)(2,1)}), bf16[8,216,128]{2,1,0:T(8,128)(2,1)}, u32[]{:S(2)}, u32[]{:S(2)}) %all-to-all-start.9) | async-done | bytes 442400 | tf_op jit(solution)/shard_map/all_to_all | solution.py:20
  196.8 2.4 fusion.25
  199.8 5.9 %collective-permute-start.7 = (bf16[56,128]{1,0:T(8,128)(2,1)S(1)}, bf16[56,128]{1,0:T(8,128)(2,1)S(1)}, u32[]{:S(2)}, u32[]{:S(2)}) collective-permute-start(bf16[56,128]{1,0:T(8,128)(2,1)S(1)} %pad_maximum_fusion.58), channel_id=1, source_target_pairs={{1,0},{16,1},{17,16},{32,17},{33,32},{48,33},{49,48},{64,49},{65,6... | collective-permute-start | bytes 43016 | tf_op jit(solution)/shard_map/ppermute | solution.py:38
  205.7 5.6 %collective-permute-start.6 = (bf16[56,128]{1,0:T(8,128)(2,1)S(1)}, bf16[56,128]{1,0:T(8,128)(2,1)S(1)}, u32[]{:S(2)}, u32[]{:S(2)}) collective-permute-start(bf16[56,128]{1,0:T(8,128)(2,1)S(1)} %pad_maximum_fusion.57), channel_id=1, source_target_pairs={{0,1},{1,16},{16,17},{17,32},{32,33},{33,48},{48,49},{49,64},{64,6... | collective-permute-start | bytes 43016 | tf_op jit(solution)/shard_map/ppermute | solution.py:34
  213.1 4.0 all-to-all-start.15
  220.4 3.6 all-to-all-start.12
  226.2 11.7 %all-to-all-done.12 = bf16[8,184,128]{2,1,0:T(8,128)(2,1)S(1)} async-done(((bf16[8,184,128]{2,1,0:T(8,128)(2,1)}), bf16[8,184,128]{2,1,0:T(8,128)(2,1)S(1)}, u32[]{:S(2)}, u32[]{:S(2)}) %all-to-all-start.12) | async-done | bytes 376864 | tf_op jit(solution)/shard_map/all_to_all | solution.py:20
  238.7 3.4 all-to-all-start.10
  246.7 6.9 %all-to-all-done.10 = bf16[8,160,128]{2,1,0:T(8,128)(2,1)S(1)} async-done(((bf16[8,160,128]{2,1,0:T(8,128)(2,1)}), bf16[8,160,128]{2,1,0:T(8,128)(2,1)S(1)}, u32[]{:S(2)}, u32[]{:S(2)}) %all-to-all-start.10) | async-done | bytes 327712 | tf_op jit(solution)/shard_map/all_to_all | solution.py:20
  253.6 3.4 all-to-all-start.13
  259.9 4.6 %collective-permute-start.11 = (bf16[2,160,1024]{2,1,0:T(8,128)(2,1)S(1)}, bf16[2,160,1024]{2,1,0:T(8,128)(2,1)}, u32[]{:S(2)}, u32[]{:S(2)}) collective-permute-start(bf16[2,160,1024]{2,1,0:T(8,128)(2,1)S(1)} %get-tuple-element.250), channel_id=1, source_target_pairs={{0,1},{1,0},{2,3},{3,2},{4,5},{5,4},{6,7},{7,6},{8,9},{9,8},{10,11... | collective-permute-start | bytes 1966088 | tf_op jit(solution)/shard_map/ppermute | solution.py:120
  268.4 7.3 %all-to-all-start.16 = ((bf16[4,32,1024]{2,1,0:T(8,128)(2,1)}), bf16[4,32,1024]{2,1,0:T(8,128)(2,1)S(1)}, u32[]{:S(2)}, u32[]{:S(2)}) async-start(bf16[4,32,1024]{2,1,0:T(8,128)(2,1)} %bitcast.127), calls=%async_computation.16 | async-start | bytes 524288 | tf_op jit(solution)/shard_map/all_to_all | solution.py:20
  277.5 3.2 all-to-all-done.16
  280.7 4.2 %all-to-all-start.14 = ((bf16[4,32,184]{2,1,0:T(8,128)(2,1)}), bf16[4,32,184]{2,1,0:T(8,128)(2,1)S(1)}, u32[]{:S(2)}, u32[]{:S(2)}) async-start(bf16[4,32,184]{2,1,0:T(8,128)(2,1)} %bitcast.63), calls=%async_computation.14 | async-start | bytes 131072 | tf_op jit(solution)/shard_map/all_to_all | solution.py:20
  286.1 2.7 bitcast_select_fusion.1
  288.8 3.6 all-to-all-start.19
  296.0 2.1 convolution_convert_fusion.1
  299.1 7.6 %all-to-all-start.17 = ((bf16[16,16,1024]{2,1,0:T(8,128)(2,1)}), bf16[16,16,1024]{2,1,0:T(8,128)(2,1)S(1)}, u32[]{:S(2)}, u32[]{:S(2)}) async-start(bf16[16,16,1024]{2,1,0:T(8,128)(2,1)} %bitcast.128), calls=%async_computation.17 | async-start | bytes 1048576 | tf_op jit(solution)/shard_map/all_to_all | solution.py:20
  307.1 15.4 %all-to-all-done.17 = bf16[16,16,1024]{2,1,0:T(8,128)(2,1)S(1)} async-done(((bf16[16,16,1024]{2,1,0:T(8,128)(2,1)}), bf16[16,16,1024]{2,1,0:T(8,128)(2,1)S(1)}, u32[]{:S(2)}, u32[]{:S(2)}) %all-to-all-start.17) | async-done | bytes 524320 | tf_op jit(solution)/shard_map/all_to_all | solution.py:20
  324.2 6.0 %all-to-all-start.18 = ((bf16[16,16,1024]{2,1,0:T(8,128)(2,1)}), bf16[16,16,1024]{2,1,0:T(8,128)(2,1)S(1)}, u32[]{:S(2)}, u32[]{:S(2)}) async-start(bf16[16,16,1024]{2,1,0:T(8,128)(2,1)} %broadcast_in_dim.1313), calls=%async_computation.18 | async-start | bytes 1048576 | tf_op jit(solution)/shard_map/all_to_all | solution.py:20
  335.3 10.2 %all-to-all-done.18 = bf16[16,16,1024]{2,1,0:T(8,128)(2,1)S(1)} async-done(((bf16[16,16,1024]{2,1,0:T(8,128)(2,1)}), bf16[16,16,1024]{2,1,0:T(8,128)(2,1)S(1)}, u32[]{:S(2)}, u32[]{:S(2)}) %all-to-all-start.18) | async-done | bytes 524320 | tf_op jit(solution)/shard_map/all_to_all | solution.py:20
  346.4 6.3 %all-to-all-start.20 = ((bf16[16,16,1024]{2,1,0:T(8,128)(2,1)}), bf16[16,16,1024]{2,1,0:T(8,128)(2,1)S(1)}, u32[]{:S(2)}, u32[]{:S(2)}) async-start(bf16[16,16,1024]{2,1,0:T(8,128)(2,1)} %bitcast.131), calls=%async_computation.20 | async-start | bytes 1048576 | tf_op jit(solution)/shard_map/all_to_all | solution.py:20
  353.7 14.3 %all-to-all-done.20 = bf16[16,16,1024]{2,1,0:T(8,128)(2,1)S(1)} async-done(((bf16[16,16,1024]{2,1,0:T(8,128)(2,1)}), bf16[16,16,1024]{2,1,0:T(8,128)(2,1)S(1)}, u32[]{:S(2)}, u32[]{:S(2)}) %all-to-all-start.20) | async-done | bytes 524320 | tf_op jit(solution)/shard_map/all_to_all | solution.py:20
  368.0 7.0 %all-to-all-start.11 = ((bf16[4,32,160]{2,1,0:T(8,128)(2,1)}), bf16[4,32,160]{2,1,0:T(8,128)(2,1)S(1)}, u32[]{:S(2)}, u32[]{:S(2)}) async-start(bf16[4,32,160]{2,1,0:T(8,128)(2,1)} %bitcast.54), calls=%async_computation.11 | async-start | bytes 131072 | tf_op jit(solution)/shard_map/all_to_all | solution.py:20
  375.9 2.4 all-to-all-done.11
  379.1 3.6 all-to-all-start.21
  383.5 15.9 %all-to-all-done.21 = bf16[16,16,1024]{2,1,0:T(8,128)(2,1)S(1)} async-done(((bf16[16,16,1024]{2,1,0:T(8,128)(2,1)}), bf16[16,16,1024]{2,1,0:T(8,128)(2,1)S(1)}, u32[]{:S(2)}, u32[]{:S(2)}) %all-to-all-start.21) | async-done | bytes 524320 | tf_op jit(solution)/shard_map/all_to_all | solution.py:20
  (489 shorter events, 94.5 us)
Async XLA Ops:
  1.5 30.5 %collective-permute-start.1 = (bf16[64,6]{1,0:T(8,128)(2,1)S(1)}, bf16[64,6]{1,0:T(8,128)(2,1)S(1)}, u32[]{:S(2)}, u32[]{:S(2)}) collective-permute-start(bf16[64,6]{1,0:T(8,128)(2,1)S(1)} %get-tuple-element.185), channel_id=1, source_target_pairs={{32,0},{64,32},{96,64},{128,96},{160,128},{192,160},{224,192},{256... | collective-permute-start | bytes 2312 | tf_op jit(solution)/shard_map/ppermute | solution.py:38
  2.8 29.2 %collective-permute-start = (bf16[64,6]{1,0:T(8,128)(2,1)S(1)}, bf16[64,6]{1,0:T(8,128)(2,1)S(1)}, u32[]{:S(2)}, u32[]{:S(2)}) collective-permute-start(bf16[64,6]{1,0:T(8,128)(2,1)S(1)} %get-tuple-element.184), channel_id=1, source_target_pairs={{0,32},{32,64},{64,96},{96,128},{128,160},{160,192},{192,224},{224... | collective-permute-start | bytes 2312 | tf_op jit(solution)/shard_map/ppermute | solution.py:34
  10.0 22.3 %all-to-all-start.5 = ((bf16[4,32,160]{2,1,0:T(8,128)(2,1)}), bf16[4,32,160]{2,1,0:T(8,128)(2,1)S(1)}, u32[]{:S(2)}, u32[]{:S(2)}) async-start(bf16[4,32,160]{2,1,0:T(8,128)(2,1)} %bitcast.574), calls=%async_computation.5 | async-start | bytes 131072 | tf_op jit(solution)/shard_map/all_to_all | solution.py:20
  23.8 101.1 %collective-permute-start.2 = (bf16[7,32,1024]{2,1,0:T(8,128)(2,1)S(1)}, bf16[7,32,1024]{2,1,0:T(8,128)(2,1)}, u32[]{:S(2)}, u32[]{:S(2)}) collective-permute-start(bf16[7,32,1024]{2,1,0:T(8,128)(2,1)S(1)} %bitcast.586), channel_id=1, source_target_pairs={{0,16},{16,0},{1,17},{17,1},{2,18},{18,2},{3,19},{19,3},{4,20},{20... | collective-permute-start | bytes 1376264 | tf_op jit(solution)/shard_map/ppermute | solution.py:120
  27.1 97.9 %collective-permute-start.4 = (bf16[7,32,1024]{2,1,0:T(8,128)(2,1)S(1)}, bf16[7,32,1024]{2,1,0:T(8,128)(2,1)}, u32[]{:S(2)}, u32[]{:S(2)}) collective-permute-start(bf16[7,32,1024]{2,1,0:T(8,128)(2,1)S(1)} %bitcast.588), channel_id=1, source_target_pairs={{0,16},{16,0},{1,17},{17,1},{2,18},{18,2},{3,19},{19,3},{4,20},{20... | collective-permute-start | bytes 1376264 | tf_op jit(solution)/shard_map/ppermute | solution.py:120
  31.9 30.7 %copy-start.18 = (s32[3]{0:T(128)}, s32[3]{0:T(128)S(1)}, u32[]{:S(2)}) copy-start(s32[3]{0:T(128)S(1)} %bitcast_subtract_fusion) | copy-start | bytes 40
  33.2 23.5 %all-to-all-start = ((bf16[32,64,92]{2,1,0:T(8,128)(2,1)}), bf16[32,64,92]{2,1,0:T(8,128)(2,1)S(1)}, u32[]{:S(2)}, u32[]{:S(2)}) async-start(bf16[32,64,92]{2,1,0:T(8,128)(2,1)} %broadcast_in_dim.1202), calls=%async_computation | async-start | bytes 1048576 | tf_op jit(solution)/shard_map/all_to_all | solution.py:20
  42.4 39.3 %copy-start.12 = (bf16[16,32,128]{2,1,0:T(8,128)(2,1)S(1)}, bf16[16,32,128]{2,1,0:T(8,128)(2,1)}, u32[]{:S(2)}) copy-start(bf16[16,32,128]{2,1,0:T(8,128)(2,1)} %param.12) | copy-start | bytes 393220
  57.5 12.2 %all-to-all-start.4 = ((bf16[4,2,32,1024]{3,2,1,0:T(8,128)(2,1)}), bf16[4,2,32,1024]{3,2,1,0:T(8,128)(2,1)S(1)}, u32[]{:S(2)}, u32[]{:S(2)}) async-start(bf16[4,2,32,1024]{3,2,1,0:T(8,128)(2,1)} %broadcast_in_dim.1208), calls=%async_computation.4 | async-start | bytes 1048576 | tf_op jit(solution)/shard_map/all_to_all | solution.py:20
  69.7 12.0 %all-to-all-start.1 = ((bf16[4,512,92]{1,2,0:T(8,128)(2,1)}), bf16[4,512,92]{1,2,0:T(8,128)(2,1)S(1)}, u32[]{:S(2)}, u32[]{:S(2)}) async-start(bf16[4,512,92]{1,2,0:T(8,128)(2,1)} %copy.80), calls=%async_computation.1 | async-start | bytes 786432 | tf_op jit(solution)/shard_map/all_to_all | solution.py:20
  82.5 18.4 %all-to-all-start.2 = ((bf16[4,512,128]{2,1,0:T(8,128)(2,1)}), bf16[4,512,128]{2,1,0:T(8,128)(2,1)S(1)}, u32[]{:S(2)}, u32[]{:S(2)}) async-start(bf16[4,512,128]{2,1,0:T(8,128)(2,1)} %broadcast_in_dim.1204), calls=%async_computation.2 | async-start | bytes 1048576 | tf_op jit(solution)/shard_map/all_to_all | solution.py:20
  100.9 14.4 %all-to-all-start.6 = ((bf16[8,160,128]{2,1,0:T(8,128)(2,1)}), bf16[8,160,128]{2,1,0:T(8,128)(2,1)S(1)}, u32[]{:S(2)}, u32[]{:S(2)}) async-start(bf16[8,160,128]{2,1,0:T(8,128)(2,1)} %bitcast.573), calls=%async_computation.6 | async-start | bytes 655360 | tf_op jit(solution)/shard_map/all_to_all | solution.py:20
  115.3 17.3 %all-to-all-start.3 = ((bf16[16,33,256]{2,1,0:T(8,128)(2,1)}), bf16[16,33,256]{2,1,0:T(8,128)(2,1)S(1)}, u32[]{:S(2)}, u32[]{:S(2)}) async-start(bf16[16,33,256]{2,1,0:T(8,128)(2,1)} %constant_dynamic-update-slice_fusion), calls=%async_computation.3 | async-start | bytes 655360 | tf_op jit(solution)/shard_map/all_to_all | solution.py:20
  126.4 17.2 %collective-permute-start.3 = (bf16[7,2,32,1024]{3,2,1,0:T(8,128)(2,1)S(1)}, bf16[7,2,32,1024]{3,2,1,0:T(8,128)(2,1)}, u32[]{:S(2)}, u32[]{:S(2)}) collective-permute-start(bf16[7,2,32,1024]{3,2,1,0:T(8,128)(2,1)S(1)} %get-tuple-element.254), channel_id=1, source_target_pairs={{0,1},{1,0},{2,3},{3,2},{4,5},{5,4},{6,7},{7,6},{8,9},{9,8},{10,11... | collective-permute-start | bytes 2752520 | tf_op jit(solution)/shard_map/ppermute | solution.py:120
  128.4 15.2 %collective-permute-start.5 = (bf16[7,2,32,1024]{3,2,1,0:T(8,128)(2,1)S(1)}, bf16[7,2,32,1024]{3,2,1,0:T(8,128)(2,1)}, u32[]{:S(2)}, u32[]{:S(2)}) collective-permute-start(bf16[7,2,32,1024]{3,2,1,0:T(8,128)(2,1)S(1)} %get-tuple-element.255), channel_id=1, source_target_pairs={{0,1},{1,0},{2,3},{3,2},{4,5},{5,4},{6,7},{7,6},{8,9},{9,8},{10,11... | collective-permute-start | bytes 2752520 | tf_op jit(solution)/shard_map/ppermute | solution.py:120
  134.9 21.8 %all-to-all-start.7 = ((bf16[8,240,128]{2,1,0:T(8,128)(2,1)}), bf16[8,240,128]{2,1,0:T(8,128)(2,1)S(1)}, u32[]{:S(2)}, u32[]{:S(2)}) async-start(bf16[8,240,128]{2,1,0:T(8,128)(2,1)} %broadcast_in_dim.1211), calls=%async_computation.7 | async-start | bytes 983040 | tf_op jit(solution)/shard_map/all_to_all | solution.py:20
  160.5 17.4 %all-to-all-start.8 = ((bf16[8,216,128]{2,1,0:T(8,128)(2,1)}), bf16[8,216,128]{2,1,0:T(8,128)(2,1)S(1)}, u32[]{:S(2)}, u32[]{:S(2)}) async-start(bf16[8,216,128]{2,1,0:T(8,128)(2,1)} %broadcast_in_dim.1225), calls=%async_computation.8 | async-start | bytes 884736 | tf_op jit(solution)/shard_map/all_to_all | solution.py:20
  180.0 16.9 %all-to-all-start.9 = ((bf16[8,216,128]{2,1,0:T(8,128)(2,1)}), bf16[8,216,128]{2,1,0:T(8,128)(2,1)}, u32[]{:S(2)}, u32[]{:S(2)}) async-start(bf16[8,216,128]{2,1,0:T(8,128)(2,1)} %broadcast_in_dim.1228), calls=%async_computation.9 | async-start | bytes 884736 | tf_op jit(solution)/shard_map/all_to_all | solution.py:20
  199.8 11.5 %collective-permute-start.7 = (bf16[56,128]{1,0:T(8,128)(2,1)S(1)}, bf16[56,128]{1,0:T(8,128)(2,1)S(1)}, u32[]{:S(2)}, u32[]{:S(2)}) collective-permute-start(bf16[56,128]{1,0:T(8,128)(2,1)S(1)} %pad_maximum_fusion.58), channel_id=1, source_target_pairs={{1,0},{16,1},{17,16},{32,17},{33,32},{48,33},{49,48},{64,49},{65,6... | collective-permute-start | bytes 43016 | tf_op jit(solution)/shard_map/ppermute | solution.py:38
  205.7 6.4 %collective-permute-start.6 = (bf16[56,128]{1,0:T(8,128)(2,1)S(1)}, bf16[56,128]{1,0:T(8,128)(2,1)S(1)}, u32[]{:S(2)}, u32[]{:S(2)}) collective-permute-start(bf16[56,128]{1,0:T(8,128)(2,1)S(1)} %pad_maximum_fusion.57), channel_id=1, source_target_pairs={{0,1},{1,16},{16,17},{17,32},{32,33},{33,48},{48,49},{49,64},{64,6... | collective-permute-start | bytes 43016 | tf_op jit(solution)/shard_map/ppermute | solution.py:34
  213.1 7.2 %all-to-all-start.15 = ((bf16[4,32,216]{2,1,0:T(8,128)(2,1)}), bf16[4,32,216]{2,1,0:T(8,128)(2,1)S(1)}, u32[]{:S(2)}, u32[]{:S(2)}) async-start(bf16[4,32,216]{2,1,0:T(8,128)(2,1)} %bitcast.95), calls=%async_computation.15 | async-start | bytes 131072 | tf_op jit(solution)/shard_map/all_to_all | solution.py:20
  220.4 24.9 %copy-start.15 = (f32[216,128]{1,0:T(8,128)S(1)}, f32[216,128]{1,0:T(8,128)}, u32[]{:S(2)}) copy-start(f32[216,128]{1,0:T(8,128)} %get-tuple-element.268) | copy-start | bytes 331780
  220.4 24.9 %copy-start.122 = (f32[128]{0:T(128)S(1)}, f32[128]{0:T(128)}, u32[]{:S(2)}) copy-start(f32[128]{0:T(128)} %broadcast_multiply_fusion.1) | copy-start | bytes 1540
  220.4 25.3 %copy-start.6 = (bf16[1,4,32,1024]{3,2,0,1:T(8,128)(2,1)S(1)}, bf16[1,4,32,1024]{3,2,0,1:T(8,128)(2,1)}, u32[]{:S(2)}) copy-start(bf16[1,4,32,1024]{3,2,0,1:T(8,128)(2,1)} %get-tuple-element.102) | copy-start | bytes 786436
  220.4 17.5 %all-to-all-start.12 = ((bf16[8,184,128]{2,1,0:T(8,128)(2,1)}), bf16[8,184,128]{2,1,0:T(8,128)(2,1)S(1)}, u32[]{:S(2)}, u32[]{:S(2)}) async-start(bf16[8,184,128]{2,1,0:T(8,128)(2,1)} %bitcast.571), calls=%async_computation.12 | async-start | bytes 753664 | tf_op jit(solution)/shard_map/all_to_all | solution.py:20
  224.0 33.8 %collective-permute-start.8 = (bf16[160,1024]{1,0:T(8,128)(2,1)S(1)}, bf16[160,1024]{1,0:T(8,128)(2,1)S(1)}, u32[]{:S(2)}, u32[]{:S(2)}) collective-permute-start(bf16[160,1024]{1,0:T(8,128)(2,1)S(1)} %copy_bitcast_fusion.1), channel_id=1, source_target_pairs={{0,16},{16,0},{1,17},{17,1},{2,18},{18,2},{3,19},{19,3},{4,20},{20... | collective-permute-start | bytes 983048 | tf_op jit(solution)/shard_map/ppermute | solution.py:120
  238.7 14.9 %all-to-all-start.10 = ((bf16[8,160,128]{2,1,0:T(8,128)(2,1)}), bf16[8,160,128]{2,1,0:T(8,128)(2,1)S(1)}, u32[]{:S(2)}, u32[]{:S(2)}) async-start(bf16[8,160,128]{2,1,0:T(8,128)(2,1)} %broadcast_in_dim.1240), calls=%async_computation.10 | async-start | bytes 655360 | tf_op jit(solution)/shard_map/all_to_all | solution.py:20
  243.2 15.4 %collective-permute-start.10 = (bf16[160,1024]{1,0:T(8,128)(2,1)S(1)}, bf16[160,1024]{1,0:T(8,128)(2,1)}, u32[]{:S(2)}, u32[]{:S(2)}) collective-permute-start(bf16[160,1024]{1,0:T(8,128)(2,1)S(1)} %copy_bitcast_fusion), channel_id=1, source_target_pairs={{0,16},{16,0},{1,17},{17,1},{2,18},{18,2},{3,19},{19,3},{4,20},{20... | collective-permute-start | bytes 983048 | tf_op jit(solution)/shard_map/ppermute | solution.py:120
  253.6 14.8 %all-to-all-start.13 = ((bf16[8,184,128]{2,1,0:T(8,128)(2,1)}), bf16[8,184,128]{2,1,0:T(8,128)(2,1)S(1)}, u32[]{:S(2)}, u32[]{:S(2)}) async-start(bf16[8,184,128]{2,1,0:T(8,128)(2,1)} %bitcast.569), calls=%async_computation.13 | async-start | bytes 753664 | tf_op jit(solution)/shard_map/all_to_all | solution.py:20
  257.8 27.1 %copy-start.8 = (bf16[8,216,128]{2,1,0:T(8,128)(2,1)S(1)}, bf16[8,216,128]{2,1,0:T(8,128)(2,1)}, u32[]{:S(2)}) copy-start(bf16[8,216,128]{2,1,0:T(8,128)(2,1)} %copy-done.7) | copy-start | bytes 1327108
  259.9 26.2 %collective-permute-start.11 = (bf16[2,160,1024]{2,1,0:T(8,128)(2,1)S(1)}, bf16[2,160,1024]{2,1,0:T(8,128)(2,1)}, u32[]{:S(2)}, u32[]{:S(2)}) collective-permute-start(bf16[2,160,1024]{2,1,0:T(8,128)(2,1)S(1)} %get-tuple-element.250), channel_id=1, source_target_pairs={{0,1},{1,0},{2,3},{3,2},{4,5},{5,4},{6,7},{7,6},{8,9},{9,8},{10,11... | collective-permute-start | bytes 1966088 | tf_op jit(solution)/shard_map/ppermute | solution.py:120
  264.5 21.6 %collective-permute-start.9 = (bf16[2,160,1024]{2,1,0:T(8,128)(2,1)S(1)}, bf16[2,160,1024]{2,1,0:T(8,128)(2,1)}, u32[]{:S(2)}, u32[]{:S(2)}) collective-permute-start(bf16[2,160,1024]{2,1,0:T(8,128)(2,1)S(1)} %get-tuple-element.251), channel_id=1, source_target_pairs={{0,1},{1,0},{2,3},{3,2},{4,5},{5,4},{6,7},{7,6},{8,9},{9,8},{10,11... | collective-permute-start | bytes 1966088 | tf_op jit(solution)/shard_map/ppermute | solution.py:120
  268.4 12.3 %all-to-all-start.16 = ((bf16[4,32,1024]{2,1,0:T(8,128)(2,1)}), bf16[4,32,1024]{2,1,0:T(8,128)(2,1)S(1)}, u32[]{:S(2)}, u32[]{:S(2)}) async-start(bf16[4,32,1024]{2,1,0:T(8,128)(2,1)} %bitcast.127), calls=%async_computation.16 | async-start | bytes 524288 | tf_op jit(solution)/shard_map/all_to_all | solution.py:20
  280.7 8.1 %all-to-all-start.14 = ((bf16[4,32,184]{2,1,0:T(8,128)(2,1)}), bf16[4,32,184]{2,1,0:T(8,128)(2,1)S(1)}, u32[]{:S(2)}, u32[]{:S(2)}) async-start(bf16[4,32,184]{2,1,0:T(8,128)(2,1)} %bitcast.63), calls=%async_computation.14 | async-start | bytes 131072 | tf_op jit(solution)/shard_map/all_to_all | solution.py:20
  288.8 10.3 %all-to-all-start.19 = ((bf16[4,32,1024]{2,1,0:T(8,128)(2,1)}), bf16[4,32,1024]{2,1,0:T(8,128)(2,1)S(1)}, u32[]{:S(2)}, u32[]{:S(2)}) async-start(bf16[4,32,1024]{2,1,0:T(8,128)(2,1)} %bitcast.130), calls=%async_computation.19 | async-start | bytes 524288 | tf_op jit(solution)/shard_map/all_to_all | solution.py:20
  298.2 24.3 %copy-start.62 = (s32[1024]{0:T(1024)S(1)}, s32[1024]{0:T(1024)}, u32[]{:S(2)}) copy-start(s32[1024]{0:T(1024)} %copy-done.61) | copy-start | bytes 12292
  299.1 23.4 %all-to-all-start.17 = ((bf16[16,16,1024]{2,1,0:T(8,128)(2,1)}), bf16[16,16,1024]{2,1,0:T(8,128)(2,1)S(1)}, u32[]{:S(2)}, u32[]{:S(2)}) async-start(bf16[16,16,1024]{2,1,0:T(8,128)(2,1)} %bitcast.128), calls=%async_computation.17 | async-start | bytes 1048576 | tf_op jit(solution)/shard_map/all_to_all | solution.py:20
  306.7 24.1 %copy-start.75 = (pred[160]{0:T(512)(128)(4,1)S(1)}, pred[160]{0:T(512)(128)(4,1)}, u32[]{:S(2)}) copy-start(pred[160]{0:T(512)(128)(4,1)} %get-tuple-element.196) | copy-start | bytes 484
  306.8 24.1 %copy-start.79 = (pred[160]{0:T(512)(128)(4,1)S(1)}, pred[160]{0:T(512)(128)(4,1)}, u32[]{:S(2)}) copy-start(pred[160]{0:T(512)(128)(4,1)} %get-tuple-element.226) | copy-start | bytes 484
  306.8 24.1 %copy-start.83 = (pred[160]{0:T(512)(128)(4,1)S(1)}, pred[160]{0:T(512)(128)(4,1)}, u32[]{:S(2)}) copy-start(pred[160]{0:T(512)(128)(4,1)} %get-tuple-element.216) | copy-start | bytes 484
  306.9 24.7 %copy-start.74 = (pred[160]{0:T(512)(128)(4,1)S(1)}, pred[160]{0:T(512)(128)(4,1)}, u32[]{:S(2)}) copy-start(pred[160]{0:T(512)(128)(4,1)} %get-tuple-element.195) | copy-start | bytes 484
  306.9 24.7 %copy-start.78 = (pred[160]{0:T(512)(128)(4,1)S(1)}, pred[160]{0:T(512)(128)(4,1)}, u32[]{:S(2)}) copy-start(pred[160]{0:T(512)(128)(4,1)} %get-tuple-element.225) | copy-start | bytes 484
  306.9 24.7 %copy-start.80 = (pred[160]{0:T(512)(128)(4,1)S(1)}, pred[160]{0:T(512)(128)(4,1)}, u32[]{:S(2)}) copy-start(pred[160]{0:T(512)(128)(4,1)} %get-tuple-element.215) | copy-start | bytes 484
  307.0 24.6 %copy-start.84 = (pred[160]{0:T(512)(128)(4,1)S(1)}, pred[160]{0:T(512)(128)(4,1)}, u32[]{:S(2)}) copy-start(pred[160]{0:T(512)(128)(4,1)} %get-tuple-element.205) | copy-start | bytes 484
  324.2 21.4 %all-to-all-start.18 = ((bf16[16,16,1024]{2,1,0:T(8,128)(2,1)}), bf16[16,16,1024]{2,1,0:T(8,128)(2,1)S(1)}, u32[]{:S(2)}, u32[]{:S(2)}) async-start(bf16[16,16,1024]{2,1,0:T(8,128)(2,1)} %broadcast_in_dim.1313), calls=%async_computation.18 | async-start | bytes 1048576 | tf_op jit(solution)/shard_map/all_to_all | solution.py:20
  346.4 21.6 %all-to-all-start.20 = ((bf16[16,16,1024]{2,1,0:T(8,128)(2,1)}), bf16[16,16,1024]{2,1,0:T(8,128)(2,1)S(1)}, u32[]{:S(2)}, u32[]{:S(2)}) async-start(bf16[16,16,1024]{2,1,0:T(8,128)(2,1)} %bitcast.131), calls=%async_computation.20 | async-start | bytes 1048576 | tf_op jit(solution)/shard_map/all_to_all | solution.py:20
  368.0 10.2 %all-to-all-start.11 = ((bf16[4,32,160]{2,1,0:T(8,128)(2,1)}), bf16[4,32,160]{2,1,0:T(8,128)(2,1)S(1)}, u32[]{:S(2)}, u32[]{:S(2)}) async-start(bf16[4,32,160]{2,1,0:T(8,128)(2,1)} %bitcast.54), calls=%async_computation.11 | async-start | bytes 131072 | tf_op jit(solution)/shard_map/all_to_all | solution.py:20
  379.1 20.3 %all-to-all-start.21 = ((bf16[16,16,1024]{2,1,0:T(8,128)(2,1)}), bf16[16,16,1024]{2,1,0:T(8,128)(2,1)S(1)}, u32[]{:S(2)}, u32[]{:S(2)}) async-start(bf16[16,16,1024]{2,1,0:T(8,128)(2,1)} %broadcast_in_dim.1314), calls=%async_computation.21 | async-start | bytes 1048576 | tf_op jit(solution)/shard_map/all_to_all | solution.py:20
  (111 other events, 1128.0 us)
